TPU v7x, 32 devices: a whole 2x2x4 slice. The times are simulated.
32 devices in a mesh: gx: 4 (over x, core), gy: 2 (over y), gz: 4 (over z).
Axes of the slice: x: 2, y: 2, z: 4, core: 2. Of those that a mesh axis runs over, the one named last changes fastest.
Arguments:
- local_schur: float32 [1024, 1024], replicated, may hold values from -1 to 4, as said below
- block_inverse: float32 [1024, 1024], replicated, may hold values from -1 to 1, as said below
- coefficient: float32 [4, 2, 4], P('gx', 'gy', 'gz'), may hold values from 0.3 to 3
- face_index: int32 [1024], replicated, may hold values from 0 to 1023, each once
- right_side: float32 [4, 2, 4, 1024, 128], P('gx', 'gy', 'gz'), may hold values from -6 to 6
Outputs:
- solution: float32 [4, 2, 4, 1024, 128], P('gx', 'gy', 'gz')
- residual: float32 [4, 2, 4, 1024, 128], P('gx', 'gy', 'gz')
Inputs may be any that keep to these rules, and one draw needn't show every extreme that they name: `local_schur`: symmetric positive definite. `block_inverse`: symmetric positive definite.
All inputs are finite; a program needn't handle non-finite values.
Results may differ from a plain program's by a relative error of at most 0.00022.
Values sent between devices are 32-bit elements; how exact they have to be, the bound alone decides.
A program may use at most 64 MiB of HBM per device.

v0:
```python
import functools
import jax
import jax.numpy as jnp
from jax import lax
from jax.experimental import pallas as pl
from jax.experimental.pallas import tpu as pltpu
from jax.sharding import PartitionSpec as P

AXES = ("gx", "gy", "gz")
MESH = pl.DeviceIdType.MESH
F32 = jnp.float32
BF16 = jnp.bfloat16


def split(x):
    hi = x.astype(BF16)
    return hi, (x - hi.astype(F32)).astype(BF16)


def halves(x):
    hi, lo = split(x)
    return jnp.concatenate([hi, lo], axis=1)


def dot(a, b):
    return jnp.dot(a, b, preferred_element_type=F32)


def kernel(
    sizes, stages, scale_ref, index_ref, side_hbm, inv_hbm, schur_hbm, sol_ref, res_ref,
    raw, side, mats, gather, scatter, send, recv, vecs, dsend, drecv,
    copy_sem, ssem, rsem, dssem, drsem,
):
    width, cols = side.shape
    face = width // 8
    position = [lax.axis_index(name) for name in AXES]

    load_side = pltpu.make_async_copy(side_hbm, side, copy_sem.at[0])
    load_inv = pltpu.make_async_copy(inv_hbm, raw.at[0], copy_sem.at[1])
    load_schur = pltpu.make_async_copy(schur_hbm, raw.at[1], copy_sem.at[2])
    load_side.start()
    load_inv.start()
    load_schur.start()

    def peer(stage, offset):
        count = 1
        me = 0
        for axis in stage:
            count *= sizes[axis]
            me = me * sizes[axis] + position[axis]
        other = lax.rem(me + offset, count)
        device = {}
        for axis in reversed(stage):
            device[AXES[axis]] = lax.rem(other, sizes[axis])
            other = lax.div(other, sizes[axis])
        return device

    counts = []
    for stage in stages:
        count = 1
        for axis in stage:
            count *= sizes[axis]
        counts.append(count)
    bases = [sum(counts[:i]) for i in range(len(counts))]

    barrier = pltpu.get_barrier_semaphore()
    for stage, count in zip(stages, counts):
        @pl.loop(1, count)
        def _(offset, stage=stage):
            pl.semaphore_signal(
                barrier, inc=1, device_id=peer(stage, offset), device_id_type=MESH
            )

    for k in range(6):
        row = index_ref[k : k + 1, :]
        down = lax.broadcasted_iota(jnp.int32, (width, face), 0)
        scatter[:, k * face : (k + 1) * face] = jnp.where(down == row, 1.0, 0.0).astype(BF16)
        column = jnp.broadcast_to(row.astype(F32), (face, face)).T
        for m in range(width // face):
            across = (lax.broadcasted_iota(jnp.int32, (face, face), 1) + m * face).astype(F32)
            gather[k * face : (k + 1) * face, m * face : (m + 1) * face] = jnp.where(
                across == column, 1.0, 0.0
            ).astype(BF16)

    for axis in range(3):
        @pl.when(position[axis] == 0)
        def _(axis=axis):
            for step in range(5):
                recv[step, 2 * axis] = jnp.zeros((face, cols), F32)

        @pl.when(position[axis] == sizes[axis] - 1)
        def _(axis=axis):
            for step in range(5):
                recv[step, 2 * axis + 1] = jnp.zeros((face, cols), F32)

    def face_copy(step, axis, up):
        mine, theirs = (2 * axis + 1, 2 * axis) if up else (2 * axis, 2 * axis + 1)
        return pltpu.make_async_remote_copy(
            src_ref=send.at[step, mine],
            dst_ref=recv.at[step, theirs],
            send_sem=ssem.at[step, mine],
            recv_sem=rsem.at[step, theirs],
            device_id={AXES[axis]: position[axis] + (1 if up else -1)},
            device_id_type=MESH,
        )

    def post(step, vec):
        out = dot(gather[...], halves(vec))
        out = out[:, :cols] + out[:, cols:]
        for k in range(6):
            send[step, k] = out[k * face : (k + 1) * face]

    def start(step):
        for axis in range(3):
            @pl.when(position[axis] < sizes[axis] - 1)
            def _(axis=axis):
                face_copy(step, axis, True).start()

            @pl.when(position[axis] > 0)
            def _(axis=axis):
                face_copy(step, axis, False).start()

    def arrived(step):
        for axis in range(3):
            @pl.when(position[axis] > 0)
            def _(axis=axis):
                face_copy(step, axis, True).wait_recv()

            @pl.when(position[axis] < sizes[axis] - 1)
            def _(axis=axis):
                face_copy(step, axis, False).wait_recv()

        got = recv[step].reshape(6 * face, cols)
        out = dot(scatter[...], halves(got))
        return out[:, :cols] + out[:, cols:]

    def load_matrix(which):
        hi, lo = split(raw[which])
        mats[which, :width] = hi
        mats[which, width:] = lo

    def product(which, vec):
        out = dot(mats[which], halves(vec))
        return out[:width, :cols] + (out[:width, cols:] + out[width:, :cols])

    def local_dot(left, right):
        return jnp.sum(left * right, axis=0, keepdims=True)

    def sum_copy(turn, level, offset):
        slot = bases[level] + offset
        return pltpu.make_async_remote_copy(
            src_ref=dsend.at[turn, level],
            dst_ref=drecv.at[turn, slot],
            send_sem=dssem.at[turn, slot],
            recv_sem=drsem.at[turn, slot],
            device_id=peer(stages[level], offset),
            device_id_type=MESH,
        )

    def sum_start(turn, level):
        @pl.loop(1, counts[level])
        def _(offset):
            sum_copy(turn, level, offset).start()

    def sum_begin(turn, first, second):
        dsend[turn, 0] = jnp.concatenate([first, second, jnp.zeros((6, cols), F32)], axis=0)
        sum_start(turn, 0)

    def sum_end(turn):
        for level, count in enumerate(counts):
            @pl.loop(1, count)
            def _(offset, level=level):
                sum_copy(turn, level, offset).wait_recv()

            total = dsend[turn, level] + jnp.sum(
                drecv[turn, bases[level] + 1 : bases[level] + count], axis=0
            )
            if level + 1 < len(counts):
                dsend[turn, level + 1] = total
                sum_start(turn, level + 1)
        return total[0:1], total[1:2]

    scale = jnp.full((1, cols), scale_ref[0, 0], F32)
    inverse = 1.0 / scale
    rhs, pre_part, pre, img_part, img, pre2_part, pre2, img2_part = [vecs.at[i] for i in range(8)]

    load_side.wait()
    post(0, side[...])
    pl.semaphore_wait(barrier, sum(counts) - len(counts))
    start(0)
    load_inv.wait()
    load_matrix(0)
    rhs[...] = side[...] + arrived(0)
    pre_part[...] = product(0, rhs[...]) * inverse
    post(1, pre_part[...])
    start(1)
    first = local_dot(rhs[...], pre_part[...])
    load_schur.wait()
    load_matrix(1)
    pre[...] = pre_part[...] + arrived(1)
    img_part[...] = product(1, pre[...]) * scale
    post(2, img_part[...])
    start(2)
    second = local_dot(pre[...], img_part[...])
    sum_begin(0, first, second)
    img[...] = img_part[...] + arrived(2)
    pre2_part[...] = product(0, img[...]) * inverse
    post(3, pre2_part[...])
    start(3)
    pre2[...] = pre2_part[...] + arrived(3)
    img2_part[...] = product(1, pre2[...]) * scale
    norm_now, along = sum_end(0)
    alpha = norm_now / along
    res_ref[...] = rhs[...] - alpha * img[...]
    sol_ref[...] = pre[...] - alpha * pre2[...]
    sum_begin(
        1,
        local_dot(res_ref[...], pre_part[...] - alpha * pre2_part[...]),
        local_dot(sol_ref[...], img_part[...] - alpha * img2_part[...]),
    )
    post(4, img2_part[...])
    start(4)
    image2 = img[...] - alpha * (img2_part[...] + arrived(4))
    norm_next, along = sum_end(1)
    ratio = norm_next / norm_now
    alpha2 = norm_next / (along - ratio * norm_next / alpha)
    sol_ref[...] = alpha * pre[...] + alpha2 * (sol_ref[...] + ratio * pre[...])
    res_ref[...] = res_ref[...] - alpha2 * (image2 + ratio * img[...])

    for step in range(5):
        for axis in range(3):
            @pl.when(position[axis] < sizes[axis] - 1)
            def _(axis=axis):
                face_copy(step, axis, True).wait_send()

            @pl.when(position[axis] > 0)
            def _(axis=axis):
                face_copy(step, axis, False).wait_send()
    for turn in range(2):
        for level, count in enumerate(counts):
            @pl.loop(1, count)
            def _(offset, level=level):
                sum_copy(turn, level, offset).wait_send()


def on_device(local_schur, block_inverse, coefficient, face_index, right_side):
    width = local_schur.shape[0]
    face = width // 8
    cols = right_side.shape[-1]
    sizes = [lax.axis_size(name) for name in AXES]
    total = sizes[0] * sizes[1] * sizes[2]
    stages = [(0, 1, 2)] if total <= 64 else [(0,), (1,), (2,)]
    slots = total if total <= 64 else sum(sizes)
    out = jax.ShapeDtypeStruct((width, cols), F32)
    sol, res = pl.pallas_call(
        functools.partial(kernel, sizes, stages),
        out_shape=(out, out),
        in_specs=[
            pl.BlockSpec(memory_space=pltpu.SMEM),
            pl.BlockSpec(memory_space=pltpu.VMEM),
            pl.BlockSpec(memory_space=pl.ANY),
            pl.BlockSpec(memory_space=pl.ANY),
            pl.BlockSpec(memory_space=pl.ANY),
        ],
        out_specs=(pl.BlockSpec(memory_space=pltpu.VMEM), pl.BlockSpec(memory_space=pltpu.VMEM)),
        scratch_shapes=[
            pltpu.VMEM((2, width, width), F32),
            pltpu.VMEM((width, cols), F32),
            pltpu.VMEM((2, 2 * width, width), BF16),
            pltpu.VMEM((6 * face, width), BF16),
            pltpu.VMEM((width, 6 * face), BF16),
            pltpu.VMEM((5, 6, face, cols), F32),
            pltpu.VMEM((5, 6, face, cols), F32),
            pltpu.VMEM((8, width, cols), F32),
            pltpu.VMEM((2, len(stages), 8, cols), F32),
            pltpu.VMEM((2, slots, 8, cols), F32),
            pltpu.SemaphoreType.DMA((3,)),
            pltpu.SemaphoreType.DMA((5, 6)),
            pltpu.SemaphoreType.DMA((5, 6)),
            pltpu.SemaphoreType.DMA((2, slots)),
            pltpu.SemaphoreType.DMA((2, slots)),
        ],
        compiler_params=pltpu.CompilerParams(
            collective_id=0, has_side_effects=True, vmem_limit_bytes=60 * 1024 * 1024
        ),
        name="schur_pcg",
    )(
        coefficient.reshape(1, 1),
        face_index.reshape(8, face),
        right_side.reshape(width, cols),
        block_inverse,
        local_schur,
    )
    return sol.reshape(1, 1, 1, width, cols), res.reshape(1, 1, 1, width, cols)


def solution(mesh):
    placed = (P(), P(), P(*AXES), P(), P(*AXES, None, None))
    return jax.shard_map(
        on_device,
        mesh=mesh,
        in_specs=placed,
        out_specs=(P(*AXES, None, None), P(*AXES, None, None)),
        check_vma=False,
    )
```

profile of v0, /device:TPU:0, one launch (start us, length us, event | category | flops | bytes accessed | tf_op | source)
XLA Modules:
  0.0 52.6 jit_solution(9773463211394931428)
XLA Ops:
  1.3 47.6 %schur_pcg.1 = (f32[1024,128]{1,0:T(8,128)}, f32[1024,128]{1,0:T(8,128)}) custom-call(f32[1,1]{1,0:T(1,128)} %bitcast.5.scale_ref, s32[8,128]{1,0:T(8,128)} %bitcast.9, f32[1024,128]{1,0:T(8,128)} %bitcast.6, f32[1024,1024]{1,0:T(8,128)} %inv_hbm.1, f32[1024,1024]{1,0:T(8,128)} %schur_hbm.1), custom_call_target="tpu_custom_call" | custom-call | tf_op jit(solution)/shard_map/schur_pcg/pallas_call | solution.py:255
  48.9 1.9 %copy.10 = f32[1,1,1,1024,128]{4,3,2,1,0:T(8,128)} copy(f32[1,1,1,1024,128]{4,3,2,1,0:T(8,128)} %bitcast.8) | data formatting | bytes 1048576
  50.8 1.9 %copy.11 = f32[1,1,1,1024,128]{4,3,2,1,0:T(8,128)} copy(f32[1,1,1,1024,128]{4,3,2,1,0:T(8,128)} %bitcast.7) | data formatting | bytes 1048576
where the time goes:
time: 52.9 us; the launch traced here: 52.6 us
  Pallas kernels  47.6 us (90%)
  local copies, waits for them, and re-layouts  3.74 us (7%)
  between operations  1.29 us (2%)
    pallas_call x1, Pallas kernels, on_device(): pl.pallas_call(functools.partial(kernel, sizes, stages), out_shape=(out,...  47.6 us
    unnamed x2, local copies, waits for them, and re-layouts  3.74 us

commit v1 on v0

--- a/solution.py
+++ b/solution.py
@@ -27,8 +27,8 @@
 
 
 def kernel(
-    sizes, stages, scale_ref, index_ref, side_hbm, inv_hbm, schur_hbm, sol_ref, res_ref,
-    raw, side, mats, gather, scatter, send, recv, vecs, dsend, drecv,
+    sizes, stages, scale_ref, order_ref, index_ref, side_hbm, inv_hbm, schur_hbm, sol_ref, res_ref,
+    raw_inv, raw_schur, rows, side, mats, gather, scatter, fresh, send, recv, vecs, dsend, drecv,
     copy_sem, ssem, rsem, dssem, drsem,
 ):
     width, cols = side.shape
@@ -36,11 +36,25 @@
     position = [lax.axis_index(name) for name in AXES]
 
     load_side = pltpu.make_async_copy(side_hbm, side, copy_sem.at[0])
-    load_inv = pltpu.make_async_copy(inv_hbm, raw.at[0], copy_sem.at[1])
-    load_schur = pltpu.make_async_copy(schur_hbm, raw.at[1], copy_sem.at[2])
+    raw = (raw_inv, raw_schur)
+    lanes = 128
+    tiles = width // lanes
+
+    def matrix_copies(which, source):
+        return [
+            pltpu.make_async_copy(
+                source.at[:, c * lanes : (c + 1) * lanes],
+                raw[which].at[:, c, :],
+                copy_sem.at[1 + which * tiles + c],
+            )
+            for c in range(tiles)
+        ]
+
+    load_inv = matrix_copies(0, inv_hbm)
+    load_schur = matrix_copies(1, schur_hbm)
     load_side.start()
-    load_inv.start()
-    load_schur.start()
+    for copy in load_inv + load_schur:
+        copy.start()
 
     def peer(stage, offset):
         count = 1
@@ -73,8 +87,6 @@
 
     for k in range(6):
         row = index_ref[k : k + 1, :]
-        down = lax.broadcasted_iota(jnp.int32, (width, face), 0)
-        scatter[:, k * face : (k + 1) * face] = jnp.where(down == row, 1.0, 0.0).astype(BF16)
         column = jnp.broadcast_to(row.astype(F32), (face, face)).T
         for m in range(width // face):
             across = (lax.broadcasted_iota(jnp.int32, (face, face), 1) + m * face).astype(F32)
@@ -104,14 +116,20 @@
             device_id_type=MESH,
         )
 
-    def post(step, vec):
-        out = dot(gather[...], halves(vec))
+    def post_side():
+        out = dot(gather[...], halves(side[...]))
         out = out[:, :cols] + out[:, cols:]
         for k in range(6):
-            send[step, k] = out[k * face : (k + 1) * face]
-
-    def start(step):
-        for axis in range(3):
+            send[0, k] = out[k * face : (k + 1) * face]
+
+    def build_scatter():
+        for k in range(8):
+            row = index_ref[k : k + 1, :]
+            down = lax.broadcasted_iota(jnp.int32, (width, face), 0)
+            scatter[:, k * face : (k + 1) * face] = jnp.where(down == row, 1.0, 0.0).astype(BF16)
+
+    def start(step, axes):
+        for axis in axes:
             @pl.when(position[axis] < sizes[axis] - 1)
             def _(axis=axis):
                 face_copy(step, axis, True).start()
@@ -120,8 +138,8 @@
             def _(axis=axis):
                 face_copy(step, axis, False).start()
 
-    def arrived(step):
-        for axis in range(3):
+    def arrived(step, axes):
+        for axis in axes:
             @pl.when(position[axis] > 0)
             def _(axis=axis):
                 face_copy(step, axis, True).wait_recv()
@@ -130,18 +148,41 @@
             def _(axis=axis):
                 face_copy(step, axis, False).wait_recv()
 
-        got = recv[step].reshape(6 * face, cols)
-        out = dot(scatter[...], halves(got))
+        low, high = 2 * axes[0], 2 * axes[-1] + 2
+        got = recv[step, low:high].reshape((high - low) * face, cols)
+        out = dot(scatter[:, low * face : high * face], halves(got))
         return out[:, :cols] + out[:, cols:]
 
+    groups = [(2 * face, 6 * face), (0, 2 * face), (6 * face, 8 * face)]
+    starts = [0, 8 * face, 12 * face]
+
     def load_matrix(which):
-        hi, lo = split(raw[which])
-        mats[which, :width] = hi
-        mats[which, width:] = lo
-
-    def product(which, vec):
-        out = dot(mats[which], halves(vec))
-        return out[:width, :cols] + (out[:width, cols:] + out[width:, :cols])
+        @pl.loop(0, width, unroll=16)
+        def _(j):
+            rows[pl.ds(pl.multiple_of(j * tiles, tiles), tiles), :] = raw[which][order_ref[j]]
+
+        for (low, high), begin in zip(groups, starts):
+            count = high - low
+            for c in range(tiles):
+                hi, lo = split(rows[pl.ds(low * tiles + c, count, stride=tiles), :])
+                mats[which, begin : begin + count, c * lanes : (c + 1) * lanes] = hi
+                mats[which, begin + count : begin + 2 * count, c * lanes : (c + 1) * lanes] = lo
+
+    def product(which, vec, factor, step):
+        right = halves(vec)
+        for g, ((low, high), begin) in enumerate(zip(groups, starts)):
+            count = high - low
+            out = dot(mats[which, begin : begin + 2 * count], right)
+            out = (out[:count, :cols] + (out[:count, cols:] + out[count:, :cols])) * factor
+            fresh[low:high] = out
+            if g < 2:
+                for k in range(low // face, high // face):
+                    send[step, k] = out[k * face - low : (k + 1) * face - low]
+                start(step, (1, 2) if g == 0 else (0,))
+
+    def natural():
+        out = dot(scatter[...], halves(fresh[...]))
+        return out[:, :cols] + out[:, cols:]
 
     def local_dot(left, right):
         return jnp.sum(left * right, axis=0, keepdims=True)
@@ -184,31 +225,39 @@
     inverse = 1.0 / scale
     rhs, pre_part, pre, img_part, img, pre2_part, pre2, img2_part = [vecs.at[i] for i in range(8)]
 
+    yz = (1, 2)
+    x = (0,)
     load_side.wait()
-    post(0, side[...])
+    post_side()
     pl.semaphore_wait(barrier, sum(counts) - len(counts))
-    start(0)
-    load_inv.wait()
+    start(0, yz)
+    start(0, x)
+    build_scatter()
+    for copy in load_inv:
+        copy.wait()
     load_matrix(0)
-    rhs[...] = side[...] + arrived(0)
-    pre_part[...] = product(0, rhs[...]) * inverse
-    post(1, pre_part[...])
-    start(1)
+    rhs[...] = side[...] + arrived(0, x)
+    rhs[...] += arrived(0, yz)
+    product(0, rhs[...], inverse, 1)
+    pre_part[...] = natural()
     first = local_dot(rhs[...], pre_part[...])
-    load_schur.wait()
+    for copy in load_schur:
+        copy.wait()
     load_matrix(1)
-    pre[...] = pre_part[...] + arrived(1)
-    img_part[...] = product(1, pre[...]) * scale
-    post(2, img_part[...])
-    start(2)
+    pre[...] = pre_part[...] + arrived(1, x)
+    pre[...] += arrived(1, yz)
+    product(1, pre[...], scale, 2)
+    img_part[...] = natural()
     second = local_dot(pre[...], img_part[...])
     sum_begin(0, first, second)
-    img[...] = img_part[...] + arrived(2)
-    pre2_part[...] = product(0, img[...]) * inverse
-    post(3, pre2_part[...])
-    start(3)
-    pre2[...] = pre2_part[...] + arrived(3)
-    img2_part[...] = product(1, pre2[...]) * scale
+    img[...] = img_part[...] + arrived(2, x)
+    img[...] += arrived(2, yz)
+    product(0, img[...], inverse, 3)
+    pre2_part[...] = natural()
+    pre2[...] = pre2_part[...] + arrived(3, x)
+    pre2[...] += arrived(3, yz)
+    product(1, pre2[...], scale, 4)
+    img2_part[...] = natural()
     norm_now, along = sum_end(0)
     alpha = norm_now / along
     res_ref[...] = rhs[...] - alpha * img[...]
@@ -218,9 +267,8 @@
         local_dot(res_ref[...], pre_part[...] - alpha * pre2_part[...]),
         local_dot(sol_ref[...], img_part[...] - alpha * img2_part[...]),
     )
-    post(4, img2_part[...])
-    start(4)
-    image2 = img[...] - alpha * (img2_part[...] + arrived(4))
+    img2_part[...] += arrived(4, x)
+    image2 = img[...] - alpha * (img2_part[...] + arrived(4, yz))
     norm_next, along = sum_end(1)
     ratio = norm_next / norm_now
     alpha2 = norm_next / (along - ratio * norm_next / alpha)
@@ -257,6 +305,7 @@
         out_shape=(out, out),
         in_specs=[
             pl.BlockSpec(memory_space=pltpu.SMEM),
+            pl.BlockSpec(memory_space=pltpu.SMEM),
             pl.BlockSpec(memory_space=pltpu.VMEM),
             pl.BlockSpec(memory_space=pl.ANY),
             pl.BlockSpec(memory_space=pl.ANY),
@@ -264,17 +313,20 @@
         ],
         out_specs=(pl.BlockSpec(memory_space=pltpu.VMEM), pl.BlockSpec(memory_space=pltpu.VMEM)),
         scratch_shapes=[
-            pltpu.VMEM((2, width, width), F32),
+            pltpu.VMEM((width, width // 128, 128), F32),
+            pltpu.VMEM((width, width // 128, 128), F32),
+            pltpu.VMEM((width * width // 128, 128), F32),
             pltpu.VMEM((width, cols), F32),
             pltpu.VMEM((2, 2 * width, width), BF16),
             pltpu.VMEM((6 * face, width), BF16),
-            pltpu.VMEM((width, 6 * face), BF16),
+            pltpu.VMEM((width, width), BF16),
+            pltpu.VMEM((width, cols), F32),
             pltpu.VMEM((5, 6, face, cols), F32),
             pltpu.VMEM((5, 6, face, cols), F32),
             pltpu.VMEM((8, width, cols), F32),
             pltpu.VMEM((2, len(stages), 8, cols), F32),
             pltpu.VMEM((2, slots, 8, cols), F32),
-            pltpu.SemaphoreType.DMA((3,)),
+            pltpu.SemaphoreType.DMA((1 + 2 * (width // 128),)),
             pltpu.SemaphoreType.DMA((5, 6)),
             pltpu.SemaphoreType.DMA((5, 6)),
             pltpu.SemaphoreType.DMA((2, slots)),
@@ -286,6 +338,7 @@
         name="schur_pcg",
     )(
         coefficient.reshape(1, 1),
+        face_index,
         face_index.reshape(8, face),
         right_side.reshape(width, cols),
         block_inverse,

time: 52.9 us -> 48.3 us (0.913)
  Pallas kernels: 47.6 us -> 43 us
    pallas_call x1, Pallas kernels: 47.6 us -> 43 us  [on_device(): pl.pallas_call(functools.partial(kernel, sizes, stages), out_shape=(out,...]
where the time goes in v1:
time: 48.3 us; the launch traced here: 48.1 us
  Pallas kernels  43 us (89%)
  local copies, waits for them, and re-layouts  3.74 us (8%)
  between operations  1.29 us (3%)
    pallas_call x1, Pallas kernels, on_device(): pl.pallas_call(functools.partial(kernel, sizes, stages), out_shape=(out,...  43 us
    unnamed x2, local copies, waits for them, and re-layouts  3.74 us

profile of v1, /device:TPU:0, one launch (start us, length us, event | category | flops | bytes accessed | tf_op | source)
XLA Modules:
  0.0 48.1 jit_solution(5359837549081205812)
XLA Ops:
  1.3 43.0 %schur_pcg.1 = (f32[1024,128]{1,0:T(8,128)}, f32[1024,128]{1,0:T(8,128)}) custom-call(f32[1,1]{1,0:T(1,128)} %bitcast.5.scale_ref, s32[1024]{0:T(1024)} %order_ref.1, s32[8,128]{1,0:T(8,128)} %bitcast.9, f32[1024,128]{1,0:T(8,128)} %bitcast.8, f32[1024,1024]{1,0:T(8,128)} %inv_hbm.1, f32[1024,1024]{1,0:T(8,128)} %schur_hbm.1), custom_call_target="tpu_custom_call" | custom-call | tf_op jit(solution)/shard_map/schur_pcg/pallas_call | solution.py:303
  44.3 1.9 %copy.10 = f32[1,1,1,1024,128]{4,3,2,1,0:T(8,128)} copy(f32[1,1,1,1024,128]{4,3,2,1,0:T(8,128)} %bitcast.7) | data formatting | bytes 1048576
  46.2 1.9 %copy.11 = f32[1,1,1,1024,128]{4,3,2,1,0:T(8,128)} copy(f32[1,1,1,1024,128]{4,3,2,1,0:T(8,128)} %bitcast.6) | data formatting | bytes 1048576

commit v2 on v1

--- a/solution.py
+++ b/solution.py
@@ -229,10 +229,10 @@
     x = (0,)
     load_side.wait()
     post_side()
+    build_scatter()
     pl.semaphore_wait(barrier, sum(counts) - len(counts))
     start(0, yz)
     start(0, x)
-    build_scatter()
     for copy in load_inv:
         copy.wait()
     load_matrix(0)
@@ -289,6 +289,11 @@
             @pl.loop(1, count)
             def _(offset, level=level):
                 sum_copy(turn, level, offset).wait_send()
+
+
+def hand_on(sol_ref, res_ref, sol_out, res_out):
+    sol_out[...] = sol_ref[...]
+    res_out[...] = res_ref[...]
 
 
 def on_device(local_schur, block_inverse, coefficient, face_index, right_side):
@@ -344,6 +349,15 @@
         block_inverse,
         local_schur,
     )
+    block = pl.BlockSpec((width // 2, cols), lambda i: (i, 0))
+    sol, res = pl.pallas_call(
+        hand_on,
+        grid=(2,),
+        out_shape=(out, out),
+        in_specs=[block, block],
+        out_specs=(block, block),
+        name="hand_on",
+    )(sol, res)
     return sol.reshape(1, 1, 1, width, cols), res.reshape(1, 1, 1, width, cols)
 
 

time: 48.3 us -> 47 us (0.973)
  local copies, waits for them, and re-layouts: 3.74 us -> 0 us
  Pallas kernels: 43 us -> 45.5 us
    unnamed x2 -> x0, local copies, waits for them, and re-layouts: 3.74 us -> none
    pallas_call x0 -> x1, Pallas kernels: none -> 2.04 us  [on_device(): pl.pallas_call(hand_on, grid=(2,), out_shape=(out, out), in_specs=[block,...]
where the time goes in v2:
time: 47 us; the launch traced here: 46.8 us
  Pallas kernels  45.5 us (97%)
  between operations  1.28 us (3%)
    pallas_call x1, Pallas kernels, on_device(): pl.pallas_call(functools.partial(kernel, sizes, stages), out_shape=(out,...  43.4 us
    pallas_call x1, Pallas kernels, on_device(): pl.pallas_call(hand_on, grid=(2,), out_shape=(out, out), in_specs=[block,...  2.04 us

profile of v2, /device:TPU:0, one launch (start us, length us, event | category | flops | bytes accessed | tf_op | source)
XLA Modules:
  0.0 46.8 jit_solution(4521561149777638309)
XLA Ops:
  1.3 43.4 %schur_pcg.1 = (f32[1024,128]{1,0:T(8,128)}, f32[1024,128]{1,0:T(8,128)}) custom-call(f32[1,1]{1,0:T(1,128)} %bitcast.5.scale_ref, s32[1024]{0:T(1024)} %order_ref.1, s32[8,128]{1,0:T(8,128)} %bitcast.7, f32[1024,128]{1,0:T(8,128)} %bitcast.6, f32[1024,1024]{1,0:T(8,128)} %inv_hbm.1, f32[1024,1024]{1,0:T(8,128)} %schur_hbm.1), custom_call_target="tpu_custom_call" | custom-call | tf_op jit(solution)/shard_map/schur_pcg/pallas_call | solution.py:308
  44.7 2.0 %hand_on.1 = (f32[1024,128]{1,0:T(8,128)}, f32[1024,128]{1,0:T(8,128)}) custom-call(f32[1024,128]{1,0:T(8,128)} %get-tuple-element.6.sol_ref, f32[1024,128]{1,0:T(8,128)} %get-tuple-element.7.res_ref), custom_call_target="tpu_custom_call" | custom-call | tf_op jit(solution)/shard_map/hand_on/pallas_call | solution.py:353
